TPU v7x, 256 devices: a whole 4x4x8 slice. The times are simulated.
256 devices in a mesh: cluster: 4 (over x), sub: 64 (over y, z, core).
Axes of the slice: x: 4, y: 4, z: 8, core: 2. Of those that a mesh axis runs over, the one named last changes fastest.
Arguments:
- dual_ops: float32 [262144, 1024], P(('cluster', 'sub')), may hold values from -21 to 21, as said below
- boundary_solve_blocks: float32 [262144, 1024], P(('cluster', 'sub')), may hold values from -21 to 21, as said below
- rigid_images: float32 [1536, 1024], P(('cluster', 'sub')), may hold values from -0.1875 to 0.1875
- coarse_rows: float32 [1536, 1536], P(('cluster', 'sub')), may hold values from -1.5 to 1.5, as said below
- gap_raw: float32 [262144, 256], P(('cluster', 'sub')), may hold values from -12 to 12
- row_maps: int32 [256, 2, 128], P(('cluster', 'sub')), may hold values from 0 to 1023, as said below
Outputs:
- multipliers: float32 [262144, 256], P(('cluster', 'sub'))
- residual: float32 [262144, 256], P(('cluster', 'sub'))
- norms: float32 [2, 256], replicated
Inputs may be any that keep to these rules, and one draw needn't show every extreme that they name: `row_maps`: A subdomain's 2 * 128 row numbers all differ; its second list faces the first list of the next subdomain, row by row. `dual_ops`: each block of a subdomain is symmetric positive definite. `boundary_solve_blocks`: each block of a subdomain is symmetric positive definite. `coarse_rows`: Symmetric.
All inputs are finite; a program needn't handle non-finite values.
Results may differ from a plain program's by a relative error of at most 0.0003.
Values sent between devices are 32-bit elements; how exact they have to be, the bound alone decides.
No kernel may reach another device: no remote copies, remote signals or barrier semaphores. Data moves between devices by JAX's collectives and lax.ppermute only.
A program may use at most 64 MiB of HBM per device.

v0:
```python
import jax
import jax.numpy as jnp
from jax import lax
from jax.sharding import Mesh
from jax.sharding import PartitionSpec as P

ITERS = 2
CLUSTER_SUB = ("cluster", "sub_0", "sub_1", "sub_2")
SUB = ("sub_0", "sub_1", "sub_2")
finest_tier = lax.Precision.HIGHEST


def passed_along(value, axis, steps):
    count = lax.axis_size(axis)
    initial, last = (max(0, -steps), min(count, count - steps))
    return lax.ppermute(value, axis, [(source, source + steps) for source in range(initial, last)])


def from_everyone(array, axis):
    copies = jnp.broadcast_to(array, (lax.axis_size(axis), *array.shape))
    return lax.all_to_all(copies, axis, split_axis=0, concat_axis=0, tiled=True)


def laid_out(parts, dim):
    shape = list(parts.shape[1:])
    shape[dim] *= parts.shape[0]
    return jnp.moveaxis(parts, 0, dim).reshape(shape)


def gathered_copies(array, axis, dim):
    parts = from_everyone(array, axis)
    return laid_out(parts, dim)


def by_axis(array, axes):
    for axis in axes:
        array = lax.psum(array, axis)
    return array


def shards(dual_ops, boundary_solve_blocks, rigid_images, coarse_rows, gap_raw, row_maps):
    processor_count = lax.axis_size(CLUSTER_SUB)
    chain_place = lax.axis_index(CLUSTER_SUB)
    left_neighbour_rows = row_maps[0, 0]
    right_neighbour_rows = row_maps[0, 1]
    local_rows = gap_raw.shape[0]
    weight = jnp.ones((local_rows,), jnp.float32)
    weight = weight.at[left_neighbour_rows].set(
        jnp.where(chain_place > 0, 0.5, 1.0).astype(jnp.float32)
    )
    weight = weight.at[right_neighbour_rows].set(
        jnp.where(chain_place < processor_count - 1, 0.5, 1.0).astype(jnp.float32)
    )
    interface_weights = weight[:, None]

    def assemble_dual(deformation_vector):
        outgoing_right = deformation_vector[right_neighbour_rows]
        outgoing_left = deformation_vector[left_neighbour_rows]
        from_left = passed_along(outgoing_right, CLUSTER_SUB, 1)
        from_right = passed_along(outgoing_left, CLUSTER_SUB, -1)
        return (
            deformation_vector.at[left_neighbour_rows]
            .add(from_left)
            .at[right_neighbour_rows]
            .add(from_right)
        )

    def gather_onto_subdomain_vector(back_rows):
        outgoing_right = back_rows[right_neighbour_rows]
        outgoing_left = back_rows[left_neighbour_rows]
        from_left = passed_along(outgoing_right, CLUSTER_SUB, 1)
        from_right = passed_along(outgoing_left, CLUSTER_SUB, -1)
        return (
            back_rows.at[left_neighbour_rows]
            .add(from_left)
            .at[right_neighbour_rows]
            .add(from_right)
        )

    def coarse_fold(piece):
        return jnp.dot(
            coarse_rows, piece, precision=finest_tier, preferred_element_type=jnp.float32
        )

    def project(deformation_vector, partial_value):
        kernel_basis_matrix = jnp.dot(
            rigid_images,
            deformation_vector,
            precision=finest_tier,
            preferred_element_type=jnp.float32,
        )
        nearby = gathered_copies(kernel_basis_matrix, SUB, 0)
        load_amounts = coarse_fold(gathered_copies(nearby, "cluster", 0))
        total = by_axis(partial_value, CLUSTER_SUB)
        back_rows = jnp.einsum("km,kr->mr", rigid_images, load_amounts, precision=finest_tier)
        return (deformation_vector - gather_onto_subdomain_vector(back_rows), total)

    residual = assemble_dual(gap_raw)
    multipliers = jnp.zeros_like(gap_raw)
    search_direction = multipliers
    previous_norm = jnp.ones((gap_raw.shape[1],), jnp.float32)
    norm_list = []
    for iteration in range(ITERS):
        norm_part = jnp.sum(interface_weights * residual * residual, axis=0)
        projected_residual, squared_length_sum = project(residual, norm_part)
        norm_list.append(squared_length_sum)
        local_contributions = jnp.dot(
            boundary_solve_blocks,
            interface_weights * projected_residual,
            precision=finest_tier,
            preferred_element_type=jnp.float32,
        )
        smoothed = interface_weights * assemble_dual(local_contributions)
        precond_part = jnp.sum(interface_weights * projected_residual * smoothed, axis=0)
        update, precond_norm = project(smoothed, precond_part)
        if iteration == 0:
            search_direction = update
        else:
            search_direction = update + precond_norm / previous_norm * search_direction
        rigid_image = assemble_dual(
            jnp.dot(
                dual_ops,
                search_direction,
                precision=finest_tier,
                preferred_element_type=jnp.float32,
            )
        )
        bending = by_axis(
            jnp.sum(interface_weights * search_direction * rigid_image, axis=0), CLUSTER_SUB
        )
        step_size = precond_norm / bending
        multipliers = multipliers + step_size * search_direction
        residual = residual - step_size * rigid_image
        previous_norm = precond_norm
    return (multipliers, residual, jnp.stack(norm_list))


def solution(mesh):
    split = Mesh(
        mesh.devices.reshape(mesh.shape["cluster"], 4, 8, 2), ("cluster", "sub_0", "sub_1", "sub_2")
    )
    in_specs = (
        P(CLUSTER_SUB, None),
        P(CLUSTER_SUB, None),
        P(CLUSTER_SUB, None),
        P(CLUSTER_SUB, None),
        P(CLUSTER_SUB, None),
        P(CLUSTER_SUB, None, None),
    )
    out_specs = (P(CLUSTER_SUB, None), P(CLUSTER_SUB, None), P())
    return jax.shard_map(
        shards, mesh=split, in_specs=in_specs, out_specs=out_specs, check_vma=False
    )
```

profile of v0, /device:TPU:1, one launch (start us, length us, event | category | flops | bytes accessed | tf_op | source)
XLA Modules:
  0.0 553.5 jit_solution(15395506081670248507)
XLA Ops:
  2.7 4.9 collective-permute-start
  8.4 1.9 collective-permute-start.1
  12.0 2.7 collective-permute-done.1
  17.0 29.4 %all_to_all.40 = f32[64,6,256]{2,1,0:T(8,128)S(1)} all-to-all(f32[64,6,256]{2,1,0:T(8,128)S(1)} %broadcast_in_dim.25), channel_id=1, replica_groups=mesh['cluster'=4,'sub_0'=4,'sub_1'=8,'sub_2'=2] {'sub_0','sub_1','sub_2'}, dimensions={0} | all-to-all | bytes 786432 | tf_op jit(solution)/shard_map/all_to_all | solution.py:21
  46.6 24.1 %all_to_all.41 = f32[4,384,256]{2,1,0:T(8,128)S(1)} all-to-all(f32[4,384,256]{2,1,0:T(8,128)S(1)} %broadcast_in_dim.26), channel_id=1, replica_groups=mesh['cluster'=4,'sub_0'=4,'sub_1'=8,'sub_2'=2] {'cluster'}, dimensions={0} | all-to-all | bytes 3145728 | tf_op jit(solution)/shard_map/all_to_all | solution.py:21
  70.7 2.6 fusion.10
  75.4 4.1 collective-permute-start.2
  80.2 1.9 collective-permute-start.3
  86.5 13.1 %scatter_fusion.4 = f32[1024,256]{1,0:T(8,128)S(1)} fusion(f32[1024,256]{1,0:T(8,128)S(1)} %scatter_fusion.3, s32[128]{0:T(128)S(1)} %get-tuple-element.30, f32[128,256]{1,0:T(8,128)S(1)} %collective-permute-done.3), kind=kCustom, calls=%fused_computation.23 | custom fusion | flops 32768 | bytes 393728 | tf_op jit(solution)/shard_map/scatter-add | solution.py:77
  99.6 10.3 %convolution_bitcast_fusion.6 = f32[1024,256]{0,1:T(8,128)} fusion(f32[1024,1024]{1,0:T(8,128)} %param.7, f32[1024,256]{1,0:T(8,128)S(1)} %scatter_fusion.2, f32[1024,256]{1,0:T(8,128)S(1)} %scatter_fusion.4, f32[1024]{0:T(1024)S(1)} %scatter_fusion), kind=kOutput, calls=%fused_computation.46 | convolution fusion | flops 3221749760 | bytes 7344128 | tf_op jit(solution)/shard_map/dot_general | solution.py:107
  112.8 3.0 collective-permute-start.4
  120.9 2.9 collective-permute-done.5
  126.2 31.7 %all_to_all.42 = f32[64,6,256]{2,1,0:T(8,128)} all-to-all(f32[64,6,256]{2,1,0:T(8,128)S(1)} %broadcast_in_dim.27), channel_id=1, replica_groups=mesh['cluster'=4,'sub_0'=4,'sub_1'=8,'sub_2'=2] {'sub_0','sub_1','sub_2'}, dimensions={0} | all-to-all | bytes 786432 | tf_op jit(solution)/shard_map/all_to_all | solution.py:21
  160.9 23.2 %all_to_all.43 = f32[4,384,256]{2,1,0:T(8,128)S(1)} all-to-all(f32[4,384,256]{2,1,0:T(8,128)S(1)} %broadcast_in_dim.28), channel_id=1, replica_groups=mesh['cluster'=4,'sub_0'=4,'sub_1'=8,'sub_2'=2] {'cluster'}, dimensions={0} | all-to-all | bytes 3145728 | tf_op jit(solution)/shard_map/all_to_all | solution.py:21
  184.0 2.6 fusion.11
  186.6 1.9 convolution_bitcast_fusion.5
  188.6 2.5 copy.40
  191.1 2.6 gather_fusion.6
  193.7 4.1 collective-permute-start.6
  197.8 2.6 gather_fusion.7
  202.3 3.3 scatter_fusion.7
  206.9 3.7 scatter_fusion.8
  213.1 10.3 %convolution_bitcast_fusion.4 = f32[1024,256]{0,1:T(8,128)} fusion(f32[1024,256]{1,0:T(8,128)S(1)} %multiply_subtract_fusion.2, f32[1024,1024]{1,0:T(8,128)} %param.6), kind=kOutput, calls=%fused_computation.44 | convolution fusion | flops 3221225472 | bytes 6291456 | tf_op jit(solution)/shard_map/dot_general | solution.py:121
  223.3 2.5 copy.43
  225.8 2.6 gather_fusion.8
  228.5 2.4 collective-permute-start.8
  230.9 2.6 gather_fusion.9
  235.4 3.3 scatter_fusion.9
  240.0 3.3 scatter_fusion.10
  243.3 2.0 fusion
  245.4 9.1 %all-reduce.5 = (f32[256]{0:T(256)S(1)}, f32[256]{0:T(256)S(1)}) all-reduce(f32[256]{0:T(256)S(1)} %get-tuple-element.4, f32[256]{0:T(256)S(1)} %get-tuple-element.7), channel_id=1, replica_groups=mesh['cluster'=4,'sub_0'=4,'sub_1'=8,'sub_2'=2] {'cluster'}, use_global_device_ids=true, to_apply=%region_9.10 | all-reduce | flops 512 | bytes 4096 | tf_op jit(solution)/shard_map/psum | solution.py:37
  254.5 6.5 %all-reduce.3 = (f32[256]{0:T(256)S(1)}, f32[256]{0:T(256)S(1)}) all-reduce(f32[256]{0:T(256)S(1)} %get-tuple-element.21, f32[256]{0:T(256)S(1)} %get-tuple-element.22), channel_id=1, replica_groups=mesh['cluster'=4,'sub_0'=4,'sub_1'=8,'sub_2'=2] {'sub_0'}, use_global_device_ids=true, to_apply=%region_10.11 | all-reduce | flops 512 | bytes 4096 | tf_op jit(solution)/shard_map/psum | solution.py:37
  261.0 19.6 %all-reduce.1 = (f32[256]{0:T(256)S(1)}, f32[256]{0:T(256)S(1)}) all-reduce(f32[256]{0:T(256)S(1)} %get-tuple-element.16, f32[256]{0:T(256)S(1)} %get-tuple-element.17), channel_id=1, replica_groups=mesh['cluster'=4,'sub_0'=4,'sub_1'=8,'sub_2'=2] {'sub_1'}, use_global_device_ids=true, to_apply=%region_11.12 | all-reduce | flops 512 | bytes 4096 | tf_op jit(solution)/shard_map/psum | solution.py:37
  280.6 5.8 %all-reduce.7 = (f32[256]{0:T(256)S(1)}, f32[256]{0:T(256)S(1)}) all-reduce(f32[256]{0:T(256)S(1)} %get-tuple-element.11, f32[256]{0:T(256)S(1)} %get-tuple-element.12), channel_id=1, replica_groups=mesh['cluster'=4,'sub_0'=4,'sub_1'=8,'sub_2'=2] {'sub_2'}, use_global_device_ids=true, to_apply=%region_12.13 | all-reduce | flops 512 | bytes 4096 | tf_op jit(solution)/shard_map/psum | solution.py:37
  288.5 22.7 %all_to_all.44 = f32[64,6,256]{2,1,0:T(8,128)S(1)} all-to-all(f32[64,6,256]{2,1,0:T(8,128)S(1)} %broadcast_in_dim.29), channel_id=1, replica_groups=mesh['cluster'=4,'sub_0'=4,'sub_1'=8,'sub_2'=2] {'sub_0','sub_1','sub_2'}, dimensions={0} | all-to-all | bytes 786432 | tf_op jit(solution)/shard_map/all_to_all | solution.py:21
  311.4 23.1 %all_to_all.45 = f32[4,384,256]{2,1,0:T(8,128)S(1)} all-to-all(f32[4,384,256]{2,1,0:T(8,128)S(1)} %broadcast_in_dim.30), channel_id=1, replica_groups=mesh['cluster'=4,'sub_0'=4,'sub_1'=8,'sub_2'=2] {'cluster'}, dimensions={0} | all-to-all | bytes 3145728 | tf_op jit(solution)/shard_map/all_to_all | solution.py:21
  334.6 2.6 fusion.12
  339.2 3.8 collective-permute-start.10
  343.8 1.9 collective-permute-start.11
  347.5 2.7 collective-permute-done.11
  351.8 10.3 %convolution_bitcast_fusion.2 = f32[1024,256]{0,1:T(8,128)} fusion(f32[1024,1024]{1,0:T(8,128)} %param.7, f32[1024,256]{1,0:T(8,128)S(1)} %multiply_subtract_fusion.1, f32[1024,256]{1,0:T(8,128)S(1)} %scatter_fusion.12, f32[1024]{0:T(1024)S(1)} %scatter_fusion), kind=kOutput, calls=%fused_computation.42 | convolution fusion | flops 3221749760 | bytes 7344128 | tf_op jit(solution)/shard_map/dot_general | solution.py:107
  364.5 1.9 collective-permute-start.12
  367.1 2.4 collective-permute-start.13
  371.3 2.2 collective-permute-done.13
  375.9 31.6 %all_to_all.46 = f32[64,6,256]{2,1,0:T(8,128)S(1)} all-to-all(f32[64,6,256]{2,1,0:T(8,128)S(1)} %broadcast_in_dim.31), channel_id=1, replica_groups=mesh['cluster'=4,'sub_0'=4,'sub_1'=8,'sub_2'=2] {'sub_0','sub_1','sub_2'}, dimensions={0} | all-to-all | bytes 786432 | tf_op jit(solution)/shard_map/all_to_all | solution.py:21
  407.7 23.4 %all_to_all.47 = f32[4,384,256]{2,1,0:T(8,128)S(1)} all-to-all(f32[4,384,256]{2,1,0:T(8,128)S(1)} %broadcast_in_dim.32), channel_id=1, replica_groups=mesh['cluster'=4,'sub_0'=4,'sub_1'=8,'sub_2'=2] {'cluster'}, dimensions={0} | all-to-all | bytes 3145728 | tf_op jit(solution)/shard_map/all_to_all | solution.py:21
  431.0 2.6 fusion.13
  433.7 1.9 convolution_bitcast_fusion.1
  439.3 4.1 collective-permute-start.14
  443.4 1.9 collective-permute-start.15
  446.9 6.9 %psum.176 = f32[256]{0:T(256)S(1)} all-reduce(f32[256]{0:T(256)S(1)} %get-tuple-element.6), channel_id=1, replica_groups=mesh['cluster'=4,'sub_0'=4,'sub_1'=8,'sub_2'=2] {'cluster'}, use_global_device_ids=true, to_apply=%region_27.28 | all-reduce | flops 256 | bytes 2048 | tf_op jit(solution)/shard_map/psum | solution.py:37
  453.8 8.3 %psum.177 = f32[256]{0:T(256)S(1)} all-reduce(f32[256]{0:T(256)S(1)} %psum.176), channel_id=1, replica_groups=mesh['cluster'=4,'sub_0'=4,'sub_1'=8,'sub_2'=2] {'sub_0'}, use_global_device_ids=true, to_apply=%region_28.29 | all-reduce | flops 256 | bytes 2048 | tf_op jit(solution)/shard_map/psum | solution.py:37
  462.1 12.3 %psum.178 = f32[256]{0:T(256)S(1)} all-reduce(f32[256]{0:T(256)S(1)} %psum.177), channel_id=1, replica_groups=mesh['cluster'=4,'sub_0'=4,'sub_1'=8,'sub_2'=2] {'sub_1'}, use_global_device_ids=true, to_apply=%region_29.30 | all-reduce | flops 256 | bytes 2048 | tf_op jit(solution)/shard_map/psum | solution.py:37
  474.4 11.3 %psum.179 = f32[256]{0:T(256)S(1)} all-reduce(f32[256]{0:T(256)S(1)} %psum.178), channel_id=1, replica_groups=mesh['cluster'=4,'sub_0'=4,'sub_1'=8,'sub_2'=2] {'sub_2'}, use_global_device_ids=true, to_apply=%region_30.31 | all-reduce | flops 256 | bytes 2048 | tf_op jit(solution)/shard_map/psum | solution.py:37
  485.8 2.0 scatter_fusion.15
  492.1 7.1 %convolution_bitcast_fusion = f32[1024,256]{0,1:T(8,128)S(1)} fusion(f32[1024,256]{1,0:T(8,128)S(1)} %multiply_add_fusion.1, f32[1024,1024]{1,0:T(8,128)S(1)} %copy-done.6), kind=kOutput, calls=%fused_computation.40 | convolution fusion | flops 3221225472 | bytes 6291456 | tf_op jit(solution)/shard_map/dot_general | solution.py:121
  500.3 3.9 collective-permute-start.16
  504.9 1.9 collective-permute-start.17
  508.6 2.7 collective-permute-done.17
  514.5 6.6 %all-reduce.4 = (f32[256]{0:T(256)S(1)}, f32[256]{0:T(256)S(1)}, f32[256]{0:T(256)S(1)}) all-reduce(f32[256]{0:T(256)S(1)} %multiply_reduce_fusion, f32[256]{0:T(256)S(1)} %get-tuple-element.5, f32[256]{0:T(256)S(1)} %get-tuple-element.3), channel_id=1, replica_groups=mesh['cluster'=4,'sub_0'=4,'sub_1'=8,'sub_2'=2] {'cluster'}, use_global_device_ids=true, to_apply=%region_36.37 | all-reduce | flops 768 | bytes 6144 | tf_op jit(solution)/shard_map/psum | solution.py:37
  521.1 6.5 %all-reduce.2 = (f32[256]{0:T(256)S(1)}, f32[256]{0:T(256)S(1)}, f32[256]{0:T(256)S(1)}) all-reduce(f32[256]{0:T(256)S(1)} %get-tuple-element.18, f32[256]{0:T(256)S(1)} %get-tuple-element.19, f32[256]{0:T(256)S(1)} %get-tuple-element.20), channel_id=1, replica_groups=mesh['cluster'=4,'sub_0'=4,'sub_1'=8,'sub_2'=2] {'sub_0'}, use_global_device_ids=true, to_apply=%region_37.38 | all-reduce | flops 768 | bytes 6144 | tf_op jit(solution)/shard_map/psum | solution.py:37
  527.6 17.9 %all-reduce = (f32[256]{0:T(256)S(1)}, f32[256]{0:T(256)S(1)}, f32[256]{0:T(256)S(1)}) all-reduce(f32[256]{0:T(256)S(1)} %get-tuple-element.13, f32[256]{0:T(256)S(1)} %get-tuple-element.14, f32[256]{0:T(256)S(1)} %get-tuple-element.15), channel_id=1, replica_groups=mesh['cluster'=4,'sub_0'=4,'sub_1'=8,'sub_2'=2] {'sub_1'}, use_global_device_ids=true, to_apply=%region_38.39 | all-reduce | flops 768 | bytes 6144 | tf_op jit(solution)/shard_map/psum | solution.py:37
  545.5 4.1 all-reduce.6
  549.6 2.9 multiply_subtract_fusion
  (103 shorter events, 68.7 us)
Async XLA Ops:
  0.6 70.1 %copy-start = (f32[6,1536]{1,0:T(8,128)S(1)}, f32[6,1536]{1,0:T(8,128)}, u32[]{:S(2)}) copy-start(f32[6,1536]{1,0:T(8,128)} %param.9) | copy-start | bytes 110596
  0.6 1.3 copy-start.9
  2.7 7.6 %collective-permute-start = (f32[128,256]{1,0:T(8,128)S(1)}, f32[128,256]{1,0:T(8,128)S(1)}, u32[]{:S(2)}, u32[]{:S(2)}) collective-permute-start(f32[128,256]{1,0:T(8,128)S(1)} %gather_fusion), channel_id=1, source_target_pairs={{0,1},{1,2},{2,3},{3,4},{4,5},{5,6},{6,7},{7,8},{8,9},{9,10},{10,1... | collective-permute-start | bytes 393224 | tf_op jit(solution)/shard_map/ppermute | solution.py:16
  8.4 6.3 %collective-permute-start.1 = (f32[128,256]{1,0:T(8,128)S(1)}, f32[128,256]{1,0:T(8,128)S(1)}, u32[]{:S(2)}, u32[]{:S(2)}) collective-permute-start(f32[128,256]{1,0:T(8,128)S(1)} %gather_fusion.1), channel_id=1, source_target_pairs={{1,0},{2,1},{3,2},{4,3},{5,4},{6,5},{7,6},{8,7},{9,8},{10,9},{11,1... | collective-permute-start | bytes 393224 | tf_op jit(solution)/shard_map/ppermute | solution.py:16
  12.0 4.3 copy-start.8
  75.4 8.8 %collective-permute-start.2 = (f32[128,256]{1,0:T(8,128)S(1)}, f32[128,256]{1,0:T(8,128)S(1)}, u32[]{:S(2)}, u32[]{:S(2)}) collective-permute-start(f32[128,256]{1,0:T(8,128)S(1)} %gather_fusion.2), channel_id=1, source_target_pairs={{0,1},{1,2},{2,3},{3,4},{4,5},{5,6},{6,7},{7,8},{8,9},{9,10},{10,1... | collective-permute-start | bytes 393224 | tf_op jit(solution)/shard_map/ppermute | solution.py:16
  80.2 6.3 %collective-permute-start.3 = (f32[128,256]{1,0:T(8,128)S(1)}, f32[128,256]{1,0:T(8,128)S(1)}, u32[]{:S(2)}, u32[]{:S(2)}) collective-permute-start(f32[128,256]{1,0:T(8,128)S(1)} %gather_fusion.3), channel_id=1, source_target_pairs={{1,0},{2,1},{3,2},{4,3},{5,4},{6,5},{7,6},{8,7},{9,8},{10,9},{11,1... | collective-permute-start | bytes 393224 | tf_op jit(solution)/shard_map/ppermute | solution.py:16
  112.8 6.4 %collective-permute-start.4 = (f32[128,256]{1,0:T(8,128)}, f32[128,256]{1,0:T(8,128)S(1)}, u32[]{:S(2)}, u32[]{:S(2)}) collective-permute-start(f32[128,256]{1,0:T(8,128)} %gather_fusion.4), channel_id=1, source_target_pairs={{0,1},{1,2},{2,3},{3,4},{4,5},{5,6},{6,7},{7,8},{8,9},{9,10},{10,1... | collective-permute-start | bytes 393224 | tf_op jit(solution)/shard_map/ppermute | solution.py:16
  117.3 6.5 %collective-permute-start.5 = (f32[128,256]{1,0:T(8,128)}, f32[128,256]{1,0:T(8,128)S(1)}, u32[]{:S(2)}, u32[]{:S(2)}) collective-permute-start(f32[128,256]{1,0:T(8,128)} %gather_fusion.5), channel_id=1, source_target_pairs={{1,0},{2,1},{3,2},{4,3},{5,4},{6,5},{7,6},{8,7},{9,8},{10,9},{11,1... | collective-permute-start | bytes 393224 | tf_op jit(solution)/shard_map/ppermute | solution.py:16
  193.7 8.6 %collective-permute-start.6 = (f32[128,256]{1,0:T(8,128)}, f32[128,256]{1,0:T(8,128)S(1)}, u32[]{:S(2)}, u32[]{:S(2)}) collective-permute-start(f32[128,256]{1,0:T(8,128)} %gather_fusion.6), channel_id=1, source_target_pairs={{0,1},{1,2},{2,3},{3,4},{4,5},{5,6},{6,7},{7,8},{8,9},{9,10},{10,1... | collective-permute-start | bytes 393224 | tf_op jit(solution)/shard_map/ppermute | solution.py:16
  200.4 6.5 %collective-permute-start.7 = (f32[128,256]{1,0:T(8,128)}, f32[128,256]{1,0:T(8,128)S(1)}, u32[]{:S(2)}, u32[]{:S(2)}) collective-permute-start(f32[128,256]{1,0:T(8,128)} %gather_fusion.7), channel_id=1, source_target_pairs={{1,0},{2,1},{3,2},{4,3},{5,4},{6,5},{7,6},{8,7},{9,8},{10,9},{11,1... | collective-permute-start | bytes 393224 | tf_op jit(solution)/shard_map/ppermute | solution.py:16
  212.1 1.0 copy-start.3
  228.5 7.0 %collective-permute-start.8 = (f32[128,256]{1,0:T(8,128)}, f32[128,256]{1,0:T(8,128)S(1)}, u32[]{:S(2)}, u32[]{:S(2)}) collective-permute-start(f32[128,256]{1,0:T(8,128)} %gather_fusion.8), channel_id=1, source_target_pairs={{0,1},{1,2},{2,3},{3,4},{4,5},{5,6},{6,7},{7,8},{8,9},{9,10},{10,1... | collective-permute-start | bytes 393224 | tf_op jit(solution)/shard_map/ppermute | solution.py:16
  233.5 6.5 %collective-permute-start.9 = (f32[128,256]{1,0:T(8,128)}, f32[128,256]{1,0:T(8,128)S(1)}, u32[]{:S(2)}, u32[]{:S(2)}) collective-permute-start(f32[128,256]{1,0:T(8,128)} %gather_fusion.9), channel_id=1, source_target_pairs={{1,0},{2,1},{3,2},{4,3},{5,4},{6,5},{7,6},{8,7},{9,8},{10,9},{11,1... | collective-permute-start | bytes 393224 | tf_op jit(solution)/shard_map/ppermute | solution.py:16
  287.9 64.0 %copy-start.1 = (f32[1024,256]{1,0:T(8,128)}, f32[1024,256]{1,0:T(8,128)S(1)}, u32[]{:S(2)}) copy-start(f32[1024,256]{1,0:T(8,128)S(1)} %multiply_subtract_fusion.1) | copy-start | bytes 3145732
  339.2 6.5 %collective-permute-start.10 = (f32[128,256]{1,0:T(8,128)S(1)}, f32[128,256]{1,0:T(8,128)S(1)}, u32[]{:S(2)}, u32[]{:S(2)}) collective-permute-start(f32[128,256]{1,0:T(8,128)S(1)} %gather_fusion.10), channel_id=1, source_target_pairs={{0,1},{1,2},{2,3},{3,4},{4,5},{5,6},{6,7},{7,8},{8,9},{9,10},{10,1... | collective-permute-start | bytes 393224 | tf_op jit(solution)/shard_map/ppermute | solution.py:16
  343.8 6.3 %collective-permute-start.11 = (f32[128,256]{1,0:T(8,128)S(1)}, f32[128,256]{1,0:T(8,128)S(1)}, u32[]{:S(2)}, u32[]{:S(2)}) collective-permute-start(f32[128,256]{1,0:T(8,128)S(1)} %gather_fusion.11), channel_id=1, source_target_pairs={{1,0},{2,1},{3,2},{4,3},{5,4},{6,5},{7,6},{8,7},{9,8},{10,9},{11,1... | collective-permute-start | bytes 393224 | tf_op jit(solution)/shard_map/ppermute | solution.py:16
  364.5 5.1 collective-permute-start.12
  367.1 6.3 %collective-permute-start.13 = (f32[128,256]{1,0:T(8,128)S(1)}, f32[128,256]{1,0:T(8,128)S(1)}, u32[]{:S(2)}, u32[]{:S(2)}) collective-permute-start(f32[128,256]{1,0:T(8,128)S(1)} %gather_fusion.13), channel_id=1, source_target_pairs={{1,0},{2,1},{3,2},{4,3},{5,4},{6,5},{7,6},{8,7},{9,8},{10,9},{11,1... | collective-permute-start | bytes 393224 | tf_op jit(solution)/shard_map/ppermute | solution.py:16
  439.3 46.5 %collective-permute-start.14 = (f32[128,256]{1,0:T(8,128)}, f32[128,256]{1,0:T(8,128)}, u32[]{:S(2)}, u32[]{:S(2)}) collective-permute-start(f32[128,256]{1,0:T(8,128)} %gather_fusion.14), channel_id=1, source_target_pairs={{0,1},{1,2},{2,3},{3,4},{4,5},{5,6},{6,7},{7,8},{8,9},{9,10},{10,1... | collective-permute-start | bytes 393224 | tf_op jit(solution)/shard_map/ppermute | solution.py:16
  443.4 44.5 %collective-permute-start.15 = (f32[128,256]{1,0:T(8,128)S(1)}, f32[128,256]{1,0:T(8,128)S(1)}, u32[]{:S(2)}, u32[]{:S(2)}) collective-permute-start(f32[128,256]{1,0:T(8,128)S(1)} %gather_fusion.15), channel_id=1, source_target_pairs={{1,0},{2,1},{3,2},{4,3},{5,4},{6,5},{7,6},{8,7},{9,8},{10,9},{11,1... | collective-permute-start | bytes 393224 | tf_op jit(solution)/shard_map/ppermute | solution.py:16
  487.9 1.7 copy-start.4
  489.6 2.6 copy-start.6
  489.8 1.0 copy-start.7
  500.3 6.6 %collective-permute-start.16 = (f32[128,256]{1,0:T(8,128)S(1)}, f32[128,256]{1,0:T(8,128)S(1)}, u32[]{:S(2)}, u32[]{:S(2)}) collective-permute-start(f32[128,256]{1,0:T(8,128)S(1)} %gather_fusion.16), channel_id=1, source_target_pairs={{0,1},{1,2},{2,3},{3,4},{4,5},{5,6},{6,7},{7,8},{8,9},{9,10},{10,1... | collective-permute-start | bytes 393224 | tf_op jit(solution)/shard_map/ppermute | solution.py:16
  504.9 6.3 %collective-permute-start.17 = (f32[128,256]{1,0:T(8,128)S(1)}, f32[128,256]{1,0:T(8,128)S(1)}, u32[]{:S(2)}, u32[]{:S(2)}) collective-permute-start(f32[128,256]{1,0:T(8,128)S(1)} %gather_fusion.17), channel_id=1, source_target_pairs={{1,0},{2,1},{3,2},{4,3},{5,4},{6,5},{7,6},{8,7},{9,8},{10,9},{11,1... | collective-permute-start | bytes 393224 | tf_op jit(solution)/shard_map/ppermute | solution.py:16
  512.9 36.7 %copy-start.2 = (f32[1024,256]{1,0:T(8,128)S(1)}, f32[1024,256]{1,0:T(8,128)}, u32[]{:S(2)}) copy-start(f32[1024,256]{1,0:T(8,128)} %copy-done.1) | copy-start | bytes 3145732
  512.9 36.7 %copy-start.5 = (f32[1024,256]{1,0:T(8,128)S(1)}, f32[1024,256]{1,0:T(8,128)}, u32[]{:S(2)}) copy-start(f32[1024,256]{1,0:T(8,128)} %copy-done.3) | copy-start | bytes 3145732
where the time goes:
time: 563 us; the launch traced here: 553 us
  blocking collectives  324 us (58%)
  other arithmetic  60.8 us (11%)
  matrix products  56.8 us (10%)
  starting transfers between devices  49.9 us (9%)
  local copies, waits for them, and re-layouts  43.9 us (8%)
  waiting for transfers between devices  16.1 us (3%)
    all_to_all x8, blocking collectives, from_everyone(): return lax.all_to_all(copies, axis, split_axis=0, concat_axis=0, tiled=True)  209 us
    psum x12, blocking collectives, by_axis(): array = lax.psum(array, axis)  115 us
    ppermute x18, starting transfers between devices, passed_along(): lax.ppermute(value, axis, [(source, source + steps) for source in range(i...  49.9 us
    scatter-add x8, other arithmetic, gather_onto_subdomain_vector(): return back_rows.at[left_neighbour_rows].add(from_left).at[right_neighbou...  28.9 us
    dot_general x2, matrix products, shards(): jnp.dot(boundary_solve_blocks, interface_weights * projected_residual, pr...  20.6 us
    scatter-add x10, other arithmetic, assemble_dual(): return deformation_vector.at[left_neighbour_rows].add(from_left).at[right...  20.1 us
    dot_general x2, matrix products, shards(): jnp.dot(dual_ops, search_direction, precision=finest_tier, preferred_elem...  17.3 us
    ppermute x18, waiting for transfers between devices, passed_along(): lax.ppermute(value, axis, [(source, source + steps) for source in range(i...  16.1 us
  transfers between devices with their start and end apart: 18, of which 8 were waited for; matrix products, arithmetic and copies ran while one was open for 6% of the time, Pallas kernels for 0%

commit v1 on v0

--- a/solution.py
+++ b/solution.py
@@ -34,7 +34,7 @@
 
 def by_axis(array, axes):
     for axis in axes:
-        array = lax.psum(array, axis)
+        array = jnp.sum(lax.all_gather(array, axis), axis=0)
     return array
 
 

time: 563 us -> 632 us (1.12)
  blocking collectives: 324 us -> 414 us
  other arithmetic: 60.8 us -> 50 us
  matrix products: 56.8 us -> 50.2 us
    all_gather x0 -> x24, blocking collectives: none -> 205 us  [by_axis(): array = jnp.sum(lax.all_gather(array, axis), axis=0)]
    psum x12 -> x0, blocking collectives: 115 us -> none  [by_axis(): array = lax.psum(array, axis)]
    scatter-add x8, other arithmetic: 28.9 us -> 17.5 us  [gather_onto_subdomain_vector(): return back_rows.at[left_neighbour_rows].add(from_left).at[right_neighbou...]
    dot_general x4, matrix products: 10.4 us -> 3.48 us  [coarse_fold(): jnp.dot(coarse_rows, piece, precision=finest_tier, preferred_element_type...]
  transfers between devices with their start and end apart: 18 -> 18, of which waited for: 8 -> 7; matrix products, arithmetic and copies ran while one was open for 6% -> 5% of each run, Pallas kernels for 0% -> 0%
where the time goes in v1:
time: 632 us; the launch traced here: 624 us
  blocking collectives  414 us (66%)
  starting transfers between devices  50.3 us (8%)
  matrix products  50.2 us (8%)
  other arithmetic  50 us (8%)
  local copies, waits for them, and re-layouts  43.9 us (7%)
  waiting for transfers between devices  13.3 us (2%)
    all_to_all x8, blocking collectives, from_everyone(): return lax.all_to_all(copies, axis, split_axis=0, concat_axis=0, tiled=True)  209 us
    all_gather x24, blocking collectives, by_axis(): array = jnp.sum(lax.all_gather(array, axis), axis=0)  205 us
    ppermute x18, starting transfers between devices, passed_along(): lax.ppermute(value, axis, [(source, source + steps) for source in range(i...  50.3 us
    dot_general x2, matrix products, shards(): jnp.dot(boundary_solve_blocks, interface_weights * projected_residual, pr...  20.6 us
    scatter-add x10, other arithmetic, assemble_dual(): return deformation_vector.at[left_neighbour_rows].add(from_left).at[right...  20.1 us
    scatter-add x8, other arithmetic, gather_onto_subdomain_vector(): return back_rows.at[left_neighbour_rows].add(from_left).at[right_neighbou...  17.5 us
    dot_general x2, matrix products, shards(): jnp.dot(dual_ops, search_direction, precision=finest_tier, preferred_elem...  17.3 us
    ppermute x18, waiting for transfers between devices, passed_along(): lax.ppermute(value, axis, [(source, source + steps) for source in range(i...  13.3 us
  transfers between devices with their start and end apart: 18, of which 7 were waited for; matrix products, arithmetic and copies ran while one was open for 5% of the time, Pallas kernels for 0%

profile of v1, /device:TPU:1, one launch (start us, length us, event | category | flops | bytes accessed | tf_op | source)
XLA Modules:
  0.0 623.8 jit_solution(14258714310578211915)
XLA Ops:
  2.7 4.9 collective-permute-start
  12.0 2.7 collective-permute-done.1
  17.0 29.4 %all_to_all.40 = f32[64,6,256]{2,1,0:T(8,128)S(1)} all-to-all(f32[64,6,256]{2,1,0:T(8,128)S(1)} %broadcast_in_dim.25), channel_id=1, replica_groups=mesh['cluster'=4,'sub_0'=4,'sub_1'=8,'sub_2'=2] {'sub_0','sub_1','sub_2'}, dimensions={0} | all-to-all | bytes 786432 | tf_op jit(solution)/shard_map/all_to_all | solution.py:21
  46.6 24.1 %all_to_all.41 = f32[4,384,256]{2,1,0:T(8,128)S(1)} all-to-all(f32[4,384,256]{2,1,0:T(8,128)S(1)} %broadcast_in_dim.26), channel_id=1, replica_groups=mesh['cluster'=4,'sub_0'=4,'sub_1'=8,'sub_2'=2] {'cluster'}, dimensions={0} | all-to-all | bytes 3145728 | tf_op jit(solution)/shard_map/all_to_all | solution.py:21
  73.7 4.1 collective-permute-start.2
  86.7 10.3 %convolution_bitcast_fusion.6 = f32[1024,256]{0,1:T(8,128)} fusion(f32[1024,1024]{1,0:T(8,128)} %param.7, f32[1024,256]{1,0:T(8,128)S(1)} %scatter_fusion.2, f32[1024,256]{1,0:T(8,128)S(1)} %scatter_fusion.4, f32[1024]{0:T(1024)S(1)} %scatter_fusion), kind=kOutput, calls=%fused_computation.46 | convolution fusion | flops 3221749760 | bytes 7344128 | tf_op jit(solution)/shard_map/dot_general | solution.py:107
  100.0 3.0 collective-permute-start.4
  108.1 2.9 collective-permute-done.5
  113.4 31.7 %all_to_all.42 = f32[64,6,256]{2,1,0:T(8,128)} all-to-all(f32[64,6,256]{2,1,0:T(8,128)S(1)} %broadcast_in_dim.27), channel_id=1, replica_groups=mesh['cluster'=4,'sub_0'=4,'sub_1'=8,'sub_2'=2] {'sub_0','sub_1','sub_2'}, dimensions={0} | all-to-all | bytes 786432 | tf_op jit(solution)/shard_map/all_to_all | solution.py:21
  148.1 23.6 %all_to_all.43 = f32[4,384,256]{2,1,0:T(8,128)S(1)} all-to-all(f32[4,384,256]{2,1,0:T(8,128)S(1)} %broadcast_in_dim.28), channel_id=1, replica_groups=mesh['cluster'=4,'sub_0'=4,'sub_1'=8,'sub_2'=2] {'cluster'}, dimensions={0} | all-to-all | bytes 3145728 | tf_op jit(solution)/shard_map/all_to_all | solution.py:21
  172.5 2.0 convolution_bitcast_fusion.5
  174.5 2.5 copy.64
  177.0 2.6 gather_fusion.6
  179.7 4.1 collective-permute-start.6
  183.7 2.6 gather_fusion.7
  188.3 3.3 scatter_fusion.7
  192.8 3.3 scatter_fusion.8
  198.6 10.3 %convolution_bitcast_fusion.4 = f32[1024,256]{0,1:T(8,128)} fusion(f32[1024,256]{1,0:T(8,128)S(1)} %multiply_subtract_fusion.2, f32[1024,1024]{1,0:T(8,128)} %param.6), kind=kOutput, calls=%fused_computation.44 | convolution fusion | flops 3221225472 | bytes 6291456 | tf_op jit(solution)/shard_map/dot_general | solution.py:121
  208.9 2.5 copy.67
  211.4 2.6 gather_fusion.8
  214.0 2.4 collective-permute-start.8
  216.4 2.6 gather_fusion.9
  219.1 2.1 collective-permute-start.9
  221.2 3.3 scatter_fusion.9
  225.5 3.3 scatter_fusion.10
  228.9 2.0 fusion
  230.9 8.5 %all-gather.24 = f32[4,1,256]{2,1,0:T(1,128)S(1)} all-gather(f32[1,1,256]{2,1,0:T(1,128)S(1)} %bitcast.99), channel_id=2, replica_groups=mesh['cluster'=4,'sub_0'=4,'sub_1'=8,'sub_2'=2] {'cluster'}, dimensions={0}, use_global_device_ids=true | all-gather | bytes 5120 | tf_op jit(solution)/shard_map/all_gather | solution.py:37
  239.5 5.8 all-gather.25
  245.3 5.8 all-gather.28
  251.1 5.9 all-gather.29
  257.0 18.9 %all-gather.30 = f32[8,1,256]{2,1,0:T(1,128)S(1)} all-gather(f32[1,1,256]{2,1,0:T(1,128)S(1)} %bitcast.113), channel_id=8, replica_groups=mesh['cluster'=4,'sub_0'=4,'sub_1'=8,'sub_2'=2] {'sub_1'}, dimensions={0}, use_global_device_ids=true | all-gather | bytes 9216 | tf_op jit(solution)/shard_map/all_gather | solution.py:37
  275.9 9.4 %all-gather.31 = f32[2,1,256]{2,1,0:T(1,128)S(1)} all-gather(f32[1,1,256]{2,1,0:T(1,128)S(1)} %bitcast.102), channel_id=9, replica_groups=mesh['cluster'=4,'sub_0'=4,'sub_1'=8,'sub_2'=2] {'sub_2'}, dimensions={0}, use_global_device_ids=true | all-gather | bytes 3072 | tf_op jit(solution)/shard_map/all_gather | solution.py:37
  285.3 11.7 %all-gather.26 = f32[8,1,256]{2,1,0:T(1,128)S(1)} all-gather(f32[1,1,256]{2,1,0:T(1,128)S(1)} %bitcast.109), channel_id=4, replica_groups=mesh['cluster'=4,'sub_0'=4,'sub_1'=8,'sub_2'=2] {'sub_1'}, dimensions={0}, use_global_device_ids=true | all-gather | bytes 9216 | tf_op jit(solution)/shard_map/all_gather | solution.py:37
  297.0 5.4 all-gather.27
  304.6 21.9 %all_to_all.44 = f32[64,6,256]{2,1,0:T(8,128)S(1)} all-to-all(f32[64,6,256]{2,1,0:T(8,128)S(1)} %broadcast_in_dim.29), channel_id=1, replica_groups=mesh['cluster'=4,'sub_0'=4,'sub_1'=8,'sub_2'=2] {'sub_0','sub_1','sub_2'}, dimensions={0} | all-to-all | bytes 786432 | tf_op jit(solution)/shard_map/all_to_all | solution.py:21
  326.7 23.1 %all_to_all.45 = f32[4,384,256]{2,1,0:T(8,128)S(1)} all-to-all(f32[4,384,256]{2,1,0:T(8,128)S(1)} %broadcast_in_dim.30), channel_id=1, replica_groups=mesh['cluster'=4,'sub_0'=4,'sub_1'=8,'sub_2'=2] {'cluster'}, dimensions={0} | all-to-all | bytes 3145728 | tf_op jit(solution)/shard_map/all_to_all | solution.py:21
  352.8 4.1 collective-permute-start.10
  361.3 2.7 collective-permute-done.11
  365.8 10.3 %convolution_bitcast_fusion.2 = f32[1024,256]{0,1:T(8,128)} fusion(f32[1024,1024]{1,0:T(8,128)} %param.7, f32[1024,256]{1,0:T(8,128)S(1)} %multiply_subtract_fusion.1, f32[1024,256]{1,0:T(8,128)S(1)} %scatter_fusion.12, f32[1024]{0:T(1024)S(1)} %scatter_fusion), kind=kOutput, calls=%fused_computation.42 | convolution fusion | flops 3221749760 | bytes 7344128 | tf_op jit(solution)/shard_map/dot_general | solution.py:107
  381.1 2.4 collective-permute-start.13
  385.3 2.2 collective-permute-done.13
  389.9 31.6 %all_to_all.46 = f32[64,6,256]{2,1,0:T(8,128)S(1)} all-to-all(f32[64,6,256]{2,1,0:T(8,128)S(1)} %broadcast_in_dim.31), channel_id=1, replica_groups=mesh['cluster'=4,'sub_0'=4,'sub_1'=8,'sub_2'=2] {'sub_0','sub_1','sub_2'}, dimensions={0} | all-to-all | bytes 786432 | tf_op jit(solution)/shard_map/all_to_all | solution.py:21
  421.7 23.4 %all_to_all.47 = f32[4,384,256]{2,1,0:T(8,128)S(1)} all-to-all(f32[4,384,256]{2,1,0:T(8,128)S(1)} %broadcast_in_dim.32), channel_id=1, replica_groups=mesh['cluster'=4,'sub_0'=4,'sub_1'=8,'sub_2'=2] {'cluster'}, dimensions={0} | all-to-all | bytes 3145728 | tf_op jit(solution)/shard_map/all_to_all | solution.py:21
  451.7 4.1 collective-permute-start.14
  459.3 6.1 all-gather.32
  465.5 7.3 %all-gather.33 = f32[4,1,256]{2,1,0:T(1,128)S(1)} all-gather(f32[1,1,256]{2,1,0:T(1,128)S(1)} %bitcast.114), channel_id=11, replica_groups=mesh['cluster'=4,'sub_0'=4,'sub_1'=8,'sub_2'=2] {'sub_0'}, dimensions={0}, use_global_device_ids=true | all-gather | bytes 5120 | tf_op jit(solution)/shard_map/all_gather | solution.py:37
  472.8 11.9 %all-gather.34 = f32[8,1,256]{2,1,0:T(1,128)S(1)} all-gather(f32[1,1,256]{2,1,0:T(1,128)S(1)} %bitcast.115), channel_id=12, replica_groups=mesh['cluster'=4,'sub_0'=4,'sub_1'=8,'sub_2'=2] {'sub_1'}, dimensions={0}, use_global_device_ids=true | all-gather | bytes 9216 | tf_op jit(solution)/shard_map/all_gather | solution.py:37
  484.7 10.6 %all-gather.35 = f32[2,1,256]{2,1,0:T(1,128)S(1)} all-gather(f32[1,1,256]{2,1,0:T(1,128)S(1)} %bitcast.104), channel_id=13, replica_groups=mesh['cluster'=4,'sub_0'=4,'sub_1'=8,'sub_2'=2] {'sub_2'}, dimensions={0}, use_global_device_ids=true | all-gather | bytes 3072 | tf_op jit(solution)/shard_map/all_gather | solution.py:37
  495.3 2.1 scatter_fusion.15
  501.7 7.1 %convolution_bitcast_fusion = f32[1024,256]{0,1:T(8,128)S(1)} fusion(f32[1024,256]{1,0:T(8,128)S(1)} %multiply_add_fusion.1, f32[1024,1024]{1,0:T(8,128)S(1)} %copy-done.6), kind=kOutput, calls=%fused_computation.40 | convolution fusion | flops 3221225472 | bytes 6291456 | tf_op jit(solution)/shard_map/dot_general | solution.py:121
  509.8 3.9 collective-permute-start.16
  516.4 5.8 all-gather.40
  522.2 5.6 all-gather.41
  527.9 12.8 %all-gather.42 = f32[8,1,256]{2,1,0:T(1,128)S(1)} all-gather(f32[1,1,256]{2,1,0:T(1,128)S(1)} %bitcast.117), channel_id=20, replica_groups=mesh['cluster'=4,'sub_0'=4,'sub_1'=8,'sub_2'=2] {'sub_1'}, dimensions={0}, use_global_device_ids=true | all-gather | bytes 9216 | tf_op jit(solution)/shard_map/all_gather | solution.py:37
  540.7 9.7 %all-gather.43 = f32[2,1,256]{2,1,0:T(1,128)S(1)} all-gather(f32[1,1,256]{2,1,0:T(1,128)S(1)} %bitcast.105), channel_id=21, replica_groups=mesh['cluster'=4,'sub_0'=4,'sub_1'=8,'sub_2'=2] {'sub_2'}, dimensions={0}, use_global_device_ids=true | all-gather | bytes 3072 | tf_op jit(solution)/shard_map/all_gather | solution.py:37
  550.4 5.4 all-gather.44
  555.8 7.2 %all-gather.45 = f32[4,1,256]{2,1,0:T(1,128)S(1)} all-gather(f32[1,1,256]{2,1,0:T(1,128)S(1)} %bitcast.118), channel_id=23, replica_groups=mesh['cluster'=4,'sub_0'=4,'sub_1'=8,'sub_2'=2] {'sub_0'}, dimensions={0}, use_global_device_ids=true | all-gather | bytes 5120 | tf_op jit(solution)/shard_map/all_gather | solution.py:37
  563.1 11.6 %all-gather.46 = f32[8,1,256]{2,1,0:T(1,128)S(1)} all-gather(f32[1,1,256]{2,1,0:T(1,128)S(1)} %bitcast.119), channel_id=24, replica_groups=mesh['cluster'=4,'sub_0'=4,'sub_1'=8,'sub_2'=2] {'sub_1'}, dimensions={0}, use_global_device_ids=true | all-gather | bytes 9216 | tf_op jit(solution)/shard_map/all_gather | solution.py:37
  574.7 8.9 %all-gather.47 = f32[2,1,256]{2,1,0:T(1,128)S(1)} all-gather(f32[1,1,256]{2,1,0:T(1,128)S(1)} %bitcast.106), channel_id=25, replica_groups=mesh['cluster'=4,'sub_0'=4,'sub_1'=8,'sub_2'=2] {'sub_2'}, dimensions={0}, use_global_device_ids=true | all-gather | bytes 3072 | tf_op jit(solution)/shard_map/all_gather | solution.py:37
  589.2 7.0 %all-gather.36 = f32[4,1,256]{2,1,0:T(1,128)S(1)} all-gather(f32[1,1,256]{2,1,0:T(1,128)S(1)} %bitcast.101), channel_id=14, replica_groups=mesh['cluster'=4,'sub_0'=4,'sub_1'=8,'sub_2'=2] {'cluster'}, dimensions={0}, use_global_device_ids=true | all-gather | bytes 5120 | tf_op jit(solution)/shard_map/all_gather | solution.py:37
  596.2 5.2 all-gather.37
  601.5 9.9 %all-gather.38 = f32[8,1,256]{2,1,0:T(1,128)S(1)} all-gather(f32[1,1,256]{2,1,0:T(1,128)S(1)} %bitcast.121), channel_id=16, replica_groups=mesh['cluster'=4,'sub_0'=4,'sub_1'=8,'sub_2'=2] {'sub_1'}, dimensions={0}, use_global_device_ids=true | all-gather | bytes 9216 | tf_op jit(solution)/shard_map/all_gather | solution.py:37
  611.4 9.0 %all-gather.39 = f32[2,1,256]{2,1,0:T(1,128)S(1)} all-gather(f32[1,1,256]{2,1,0:T(1,128)S(1)} %bitcast.107), channel_id=17, replica_groups=mesh['cluster'=4,'sub_0'=4,'sub_1'=8,'sub_2'=2] {'sub_2'}, dimensions={0}, use_global_device_ids=true | all-gather | bytes 3072 | tf_op jit(solution)/shard_map/all_gather | solution.py:37
  620.4 2.9 multiply_subtract_fusion
  (139 shorter events, 86.5 us)
Async XLA Ops:
  0.6 70.1 %copy-start = (f32[6,1536]{1,0:T(8,128)S(1)}, f32[6,1536]{1,0:T(8,128)}, u32[]{:S(2)}) copy-start(f32[6,1536]{1,0:T(8,128)} %param.9) | copy-start | bytes 110596
  0.6 1.3 copy-start.9
  2.7 7.6 %collective-permute-start = (f32[128,256]{1,0:T(8,128)S(1)}, f32[128,256]{1,0:T(8,128)S(1)}, u32[]{:S(2)}, u32[]{:S(2)}) collective-permute-start(f32[128,256]{1,0:T(8,128)S(1)} %gather_fusion), channel_id=1, source_target_pairs={{0,1},{1,2},{2,3},{3,4},{4,5},{5,6},{6,7},{7,8},{8,9},{9,10},{10,1... | collective-permute-start | bytes 393224 | tf_op jit(solution)/shard_map/ppermute | solution.py:16
  8.4 6.3 %collective-permute-start.1 = (f32[128,256]{1,0:T(8,128)S(1)}, f32[128,256]{1,0:T(8,128)S(1)}, u32[]{:S(2)}, u32[]{:S(2)}) collective-permute-start(f32[128,256]{1,0:T(8,128)S(1)} %gather_fusion.1), channel_id=1, source_target_pairs={{1,0},{2,1},{3,2},{4,3},{5,4},{6,5},{7,6},{8,7},{9,8},{10,9},{11,1... | collective-permute-start | bytes 393224 | tf_op jit(solution)/shard_map/ppermute | solution.py:16
  12.0 4.3 copy-start.8
  73.7 8.8 %collective-permute-start.2 = (f32[128,256]{1,0:T(8,128)S(1)}, f32[128,256]{1,0:T(8,128)S(1)}, u32[]{:S(2)}, u32[]{:S(2)}) collective-permute-start(f32[128,256]{1,0:T(8,128)S(1)} %gather_fusion.2), channel_id=1, source_target_pairs={{0,1},{1,2},{2,3},{3,4},{4,5},{5,6},{6,7},{7,8},{8,9},{9,10},{10,1... | collective-permute-start | bytes 393224 | tf_op jit(solution)/shard_map/ppermute | solution.py:16
  78.6 6.3 %collective-permute-start.3 = (f32[128,256]{1,0:T(8,128)S(1)}, f32[128,256]{1,0:T(8,128)S(1)}, u32[]{:S(2)}, u32[]{:S(2)}) collective-permute-start(f32[128,256]{1,0:T(8,128)S(1)} %gather_fusion.3), channel_id=1, source_target_pairs={{1,0},{2,1},{3,2},{4,3},{5,4},{6,5},{7,6},{8,7},{9,8},{10,9},{11,1... | collective-permute-start | bytes 393224 | tf_op jit(solution)/shard_map/ppermute | solution.py:16
  100.0 6.4 %collective-permute-start.4 = (f32[128,256]{1,0:T(8,128)}, f32[128,256]{1,0:T(8,128)S(1)}, u32[]{:S(2)}, u32[]{:S(2)}) collective-permute-start(f32[128,256]{1,0:T(8,128)} %gather_fusion.4), channel_id=1, source_target_pairs={{0,1},{1,2},{2,3},{3,4},{4,5},{5,6},{6,7},{7,8},{8,9},{9,10},{10,1... | collective-permute-start | bytes 393224 | tf_op jit(solution)/shard_map/ppermute | solution.py:16
  104.4 6.5 %collective-permute-start.5 = (f32[128,256]{1,0:T(8,128)}, f32[128,256]{1,0:T(8,128)S(1)}, u32[]{:S(2)}, u32[]{:S(2)}) collective-permute-start(f32[128,256]{1,0:T(8,128)} %gather_fusion.5), channel_id=1, source_target_pairs={{1,0},{2,1},{3,2},{4,3},{5,4},{6,5},{7,6},{8,7},{9,8},{10,9},{11,1... | collective-permute-start | bytes 393224 | tf_op jit(solution)/shard_map/ppermute | solution.py:16
  179.7 8.6 %collective-permute-start.6 = (f32[128,256]{1,0:T(8,128)}, f32[128,256]{1,0:T(8,128)S(1)}, u32[]{:S(2)}, u32[]{:S(2)}) collective-permute-start(f32[128,256]{1,0:T(8,128)} %gather_fusion.6), channel_id=1, source_target_pairs={{0,1},{1,2},{2,3},{3,4},{4,5},{5,6},{6,7},{7,8},{8,9},{9,10},{10,1... | collective-permute-start | bytes 393224 | tf_op jit(solution)/shard_map/ppermute | solution.py:16
  186.3 6.5 %collective-permute-start.7 = (f32[128,256]{1,0:T(8,128)}, f32[128,256]{1,0:T(8,128)S(1)}, u32[]{:S(2)}, u32[]{:S(2)}) collective-permute-start(f32[128,256]{1,0:T(8,128)} %gather_fusion.7), channel_id=1, source_target_pairs={{1,0},{2,1},{3,2},{4,3},{5,4},{6,5},{7,6},{8,7},{9,8},{10,9},{11,1... | collective-permute-start | bytes 393224 | tf_op jit(solution)/shard_map/ppermute | solution.py:16
  197.6 1.0 copy-start.3
  214.0 7.1 %collective-permute-start.8 = (f32[128,256]{1,0:T(8,128)}, f32[128,256]{1,0:T(8,128)S(1)}, u32[]{:S(2)}, u32[]{:S(2)}) collective-permute-start(f32[128,256]{1,0:T(8,128)} %gather_fusion.8), channel_id=1, source_target_pairs={{0,1},{1,2},{2,3},{3,4},{4,5},{5,6},{6,7},{7,8},{8,9},{9,10},{10,1... | collective-permute-start | bytes 393224 | tf_op jit(solution)/shard_map/ppermute | solution.py:16
  219.1 6.5 %collective-permute-start.9 = (f32[128,256]{1,0:T(8,128)}, f32[128,256]{1,0:T(8,128)S(1)}, u32[]{:S(2)}, u32[]{:S(2)}) collective-permute-start(f32[128,256]{1,0:T(8,128)} %gather_fusion.9), channel_id=1, source_target_pairs={{1,0},{2,1},{3,2},{4,3},{5,4},{6,5},{7,6},{8,7},{9,8},{10,9},{11,1... | collective-permute-start | bytes 393224 | tf_op jit(solution)/shard_map/ppermute | solution.py:16
  303.9 61.9 %copy-start.1 = (f32[1024,256]{1,0:T(8,128)}, f32[1024,256]{1,0:T(8,128)S(1)}, u32[]{:S(2)}) copy-start(f32[1024,256]{1,0:T(8,128)S(1)} %multiply_subtract_fusion.1) | copy-start | bytes 3145732
  352.8 6.8 %collective-permute-start.10 = (f32[128,256]{1,0:T(8,128)S(1)}, f32[128,256]{1,0:T(8,128)S(1)}, u32[]{:S(2)}, u32[]{:S(2)}) collective-permute-start(f32[128,256]{1,0:T(8,128)S(1)} %gather_fusion.10), channel_id=1, source_target_pairs={{0,1},{1,2},{2,3},{3,4},{4,5},{5,6},{6,7},{7,8},{8,9},{9,10},{10,1... | collective-permute-start | bytes 393224 | tf_op jit(solution)/shard_map/ppermute | solution.py:16
  357.6 6.3 %collective-permute-start.11 = (f32[128,256]{1,0:T(8,128)S(1)}, f32[128,256]{1,0:T(8,128)S(1)}, u32[]{:S(2)}, u32[]{:S(2)}) collective-permute-start(f32[128,256]{1,0:T(8,128)S(1)} %gather_fusion.11), channel_id=1, source_target_pairs={{1,0},{2,1},{3,2},{4,3},{5,4},{6,5},{7,6},{8,7},{9,8},{10,9},{11,1... | collective-permute-start | bytes 393224 | tf_op jit(solution)/shard_map/ppermute | solution.py:16
  378.5 5.1 collective-permute-start.12
  381.1 6.3 %collective-permute-start.13 = (f32[128,256]{1,0:T(8,128)S(1)}, f32[128,256]{1,0:T(8,128)S(1)}, u32[]{:S(2)}, u32[]{:S(2)}) collective-permute-start(f32[128,256]{1,0:T(8,128)S(1)} %gather_fusion.13), channel_id=1, source_target_pairs={{1,0},{2,1},{3,2},{4,3},{5,4},{6,5},{7,6},{8,7},{9,8},{10,9},{11,1... | collective-permute-start | bytes 393224 | tf_op jit(solution)/shard_map/ppermute | solution.py:16
  451.7 43.6 %collective-permute-start.14 = (f32[128,256]{1,0:T(8,128)}, f32[128,256]{1,0:T(8,128)}, u32[]{:S(2)}, u32[]{:S(2)}) collective-permute-start(f32[128,256]{1,0:T(8,128)} %gather_fusion.14), channel_id=1, source_target_pairs={{0,1},{1,2},{2,3},{3,4},{4,5},{5,6},{6,7},{7,8},{8,9},{9,10},{10,1... | collective-permute-start | bytes 393224 | tf_op jit(solution)/shard_map/ppermute | solution.py:16
  455.8 41.6 %collective-permute-start.15 = (f32[128,256]{1,0:T(8,128)S(1)}, f32[128,256]{1,0:T(8,128)S(1)}, u32[]{:S(2)}, u32[]{:S(2)}) collective-permute-start(f32[128,256]{1,0:T(8,128)S(1)} %gather_fusion.15), channel_id=1, source_target_pairs={{1,0},{2,1},{3,2},{4,3},{5,4},{6,5},{7,6},{8,7},{9,8},{10,9},{11,1... | collective-permute-start | bytes 393224 | tf_op jit(solution)/shard_map/ppermute | solution.py:16
  497.4 1.7 copy-start.4
  499.1 2.6 copy-start.6
  499.3 1.0 copy-start.7
  509.8 74.4 %collective-permute-start.16 = (f32[128,256]{1,0:T(8,128)S(1)}, f32[128,256]{1,0:T(8,128)S(1)}, u32[]{:S(2)}, u32[]{:S(2)}) collective-permute-start(f32[128,256]{1,0:T(8,128)S(1)} %gather_fusion.16), channel_id=1, source_target_pairs={{0,1},{1,2},{2,3},{3,4},{4,5},{5,6},{6,7},{7,8},{8,9},{9,10},{10,1... | collective-permute-start | bytes 393224 | tf_op jit(solution)/shard_map/ppermute | solution.py:16
  514.5 71.4 %collective-permute-start.17 = (f32[128,256]{1,0:T(8,128)S(1)}, f32[128,256]{1,0:T(8,128)S(1)}, u32[]{:S(2)}, u32[]{:S(2)}) collective-permute-start(f32[128,256]{1,0:T(8,128)S(1)} %gather_fusion.17), channel_id=1, source_target_pairs={{1,0},{2,1},{3,2},{4,3},{5,4},{6,5},{7,6},{8,7},{9,8},{10,9},{11,1... | collective-permute-start | bytes 393224 | tf_op jit(solution)/shard_map/ppermute | solution.py:16
  587.6 32.8 %copy-start.2 = (f32[1024,256]{1,0:T(8,128)S(1)}, f32[1024,256]{1,0:T(8,128)}, u32[]{:S(2)}) copy-start(f32[1024,256]{1,0:T(8,128)} %copy-done.1) | copy-start | bytes 3145732
  587.6 32.8 %copy-start.5 = (f32[1024,256]{1,0:T(8,128)S(1)}, f32[1024,256]{1,0:T(8,128)}, u32[]{:S(2)}) copy-start(f32[1024,256]{1,0:T(8,128)} %copy-done.3) | copy-start | bytes 3145732
